TPU v7x, 32 devices: a whole 2x2x4 slice. The times are simulated.
32 devices in a mesh: pole: 2 (over y), row: 4 (over z), col: 4 (over x, core).
Axes of the slice: x: 2, y: 2, z: 4, core: 2. Of those that a mesh axis runs over, the one named last changes fastest.
Arguments:
- ainv_cc: bfloat16 [2048, 1024], P(('pole', 'row'), 'col'), parts along dimension 0, may hold values from -6 to 6
- factor: bfloat16 [4, 1024, 1024], P('pole', 'row', 'col'), parts along dimension 0, may hold values from -0.375 to 0.375
- inv_pivot: float32 [4, 1024, 1024], P('pole', 'row', 'col'), parts along dimension 0, may hold values from -6 to 6
- pattern: int32 [2, 8], replicated, may hold values from 0 to 1, as said below
Outputs:
- ainv_kc: bfloat16 [4, 1024, 1024], P('pole', 'col', 'row'), parts along dimension 0
- ainv_kk: float32 [4, 1024, 1024], P('pole', 'row', 'col'), parts along dimension 0
There are 2 independent parts, one for each index of `pole`. A program takes and returns all parts, laid end to end along the dimension named above; an argument that names none is the same for every part. Nothing has to cross between parts.
Inputs may be any that keep to these rules, and one draw needn't show every extreme that they name: `pattern`: for each supernode, each aligned group of 2 consecutive blocks (blocks g * 2 to (g + 1) * 2 - 1) holds at most 1 nonzero blocks, and some group holds exactly 1.
All inputs are finite; a program needn't handle non-finite values.
Results may differ from a plain program's by a relative error of at most 0.012.
Values may be sent and summed in bfloat16 or wider, within the bound.
A program may use at most 64 MiB of HBM per device.

v0:
```python
import jax
import jax.numpy as jnp
from jax import lax
from jax.sharding import PartitionSpec as P

BLK = 128
SUPERS = 2
RB_DEV = 2


def spread(x, axis, root):
    mine = lax.axis_index(axis) == root
    return lax.psum(jnp.where(mine, x, jnp.zeros_like(x)), axis)


def body(ainv_cc, factor, inv_pivot, pattern):
    rows_here = factor.shape[1]
    width_part = factor.shape[2]
    per_col = lax.axis_size("row") // lax.axis_size("col")
    row_index = lax.axis_index("row")
    col_index = lax.axis_index("col")
    full_width = lax.all_gather(factor, "col", axis=2, tiled=True)
    full_cols = full_width.shape[2]
    own_marks = lax.dynamic_slice_in_dim(pattern, row_index * RB_DEV, RB_DEV, 1)
    blocks = full_width.reshape(SUPERS, RB_DEV, BLK, full_cols)
    masked = jnp.where(own_marks[:, :, None, None] > 0, blocks, jnp.zeros_like(blocks))
    local_factor = masked.reshape(SUPERS, rows_here, full_cols)
    received = []
    for section in range(per_col):
        received.append(spread(local_factor, "row", col_index * per_col + section))
    gathered_rows = jnp.concatenate(received, axis=1)
    left_list = [ainv_cc for super_index in range(SUPERS)]
    cross_list = []
    diag_list = []
    for super_index in range(SUPERS):
        rows_matrix = gathered_rows[super_index]
        operand = left_list[super_index]
        factor_rows = local_factor[super_index]

        def column_term(first_row, row_count, rows_matrix=rows_matrix, operand=operand):
            return lax.dot_general(
                rows_matrix, operand, (((0,), (1,)), ((), ())), preferred_element_type=jnp.float32
            )

        summed = lax.psum_scatter(
            column_term(jnp.int32(0), lax.axis_size("col") * width_part).astype(jnp.bfloat16),
            "col",
            scatter_dimension=0,
            tiled=True,
        ).astype(jnp.float32)
        cross_block = (-summed).astype(jnp.bfloat16)

        def diagonal_term(first_row, row_count, factor_rows=factor_rows, cross_block=cross_block):
            return lax.dot_general(
                factor_rows,
                cross_block,
                (((0,), (1,)), ((), ())),
                preferred_element_type=jnp.float32,
            )

        update = lax.psum_scatter(
            diagonal_term(
                jnp.int32(0), lax.axis_size("row") * (full_cols // lax.axis_size("row"))
            ).astype(jnp.bfloat16),
            "row",
            scatter_dimension=0,
            tiled=True,
        ).astype(jnp.float32)
        cross_list.append(cross_block)
        diag_list.append(inv_pivot[super_index] - update)
    return (jnp.stack(cross_list), jnp.stack(diag_list))


def solution(mesh):
    placed = (P(("pole", "row"), "col"), P("pole", "row", "col"), P("pole", "row", "col"), P())
    return jax.shard_map(
        body,
        mesh=mesh,
        in_specs=placed,
        out_specs=(P("pole", "col", "row"), P("pole", "row", "col")),
        check_vma=False,
    )
```

profile of v0, /device:TPU:0, one launch (start us, length us, event | category | flops | bytes accessed | tf_op | source)
XLA Modules:
  0.0 187.2 jit_solution(14719530490384037543)
XLA Ops:
  7.2 0.0 all-gather.2.cloned.1.call-start
  7.2 0.7 all-gather.2.cloned.1.call-update
  7.9 0.0 all-reduce.2.cloned.1.call-start
  8.0 0.7 copy-done.6
  8.6 0.1 dynamic-slice_compare_fusion
  8.7 0.1 broadcast_bitcast_fusion
  8.8 20.3 %all-gather.2.cloned.1.call-done = bf16[2,256,1024]{2,1,0:T(8,128)(2,1)} async-done(((bf16[2,256,256]{2,1,0:T(8,128)(2,1)}), bf16[2,256,1024]{2,1,0:T(8,128)(2,1)}) %all-gather.2.cloned.1.call-update) | async-done | bytes 1048592 | tf_op jit(solution)/shard_map/all_gather | solution.py:22
  29.1 2.4 %select_select_fusion = bf16[2,256,1024]{2,1,0:T(8,128)(2,1)} fusion(bf16[2,256,1024]{2,1,0:T(8,128)(2,1)} %all-gather.2.cloned.1.call-done, pred[2,256]{1,0:T(4,128)(4,1)S(1)} %bitcast.37, pred[]{:T(512)S(6)} %eq.3), kind=kLoop, calls=%fused_computation.4 | loop fusion | flops 1048576 | bytes 2097665 | tf_op jit(solution)/shard_map/jit(_where)/select_n | solution.py:13
  31.5 0.0 all-reduce.2.cloned.1.call-update
  31.5 0.0 reduce-scatter.7.cloned.1.call-start
  31.6 51.9 %all-reduce.2.cloned.1.call-done = bf16[2,256,1024]{2,1,0:T(8,128)(2,1)} async-done(((bf16[2,256,1024]{2,1,0:T(8,128)(2,1)}), bf16[2,256,1024]{2,1,0:T(8,128)(2,1)}) %all-reduce.2.cloned.1.call-update) | async-done | bytes 1048592 | tf_op jit(solution)/shard_map/psum | solution.py:13
  83.5 2.3 %convolution_convert_fusion.2 = bf16[1024,256]{1,0:T(8,128)(2,1)} fusion(bf16[256,256]{1,0:T(8,128)(2,1)S(1)} %copy-done, bf16[2,256,1024]{2,1,0:T(8,128)(2,1)} %all-reduce.2.cloned.1.call-done), kind=kOutput, calls=%fused_computation.2 | convolution fusion | flops 134479872 | bytes 1179648 | tf_op jit(solution)/shard_map/dot_general | solution.py:41
  85.8 0.0 reduce-scatter.7.cloned.1.call-update
  85.8 0.0 reduce-scatter.5.cloned.1.call-start
  85.9 1.2 convolution_convert_fusion.3
  87.1 0.0 reduce-scatter.5.cloned.1.call-update
  87.1 0.0 reduce-scatter.11.cloned.1.call-start
  87.1 0.1 broadcast_select_fusion
  87.3 0.1 fusion.4
  87.4 20.4 %reduce-scatter.7.cloned.1.call-done = bf16[256,256]{1,0:T(8,128)(2,1)} async-done(((bf16[1024,256]{1,0:T(8,128)(2,1)}), bf16[256,256]{1,0:T(8,128)(2,1)}) %reduce-scatter.7.cloned.1.call-update) | async-done | bytes 131088 | tf_op jit(solution)/shard_map/reduce_scatter | solution.py:45
  107.8 2.1 %convolution_convert_fusion = bf16[1024,256]{1,0:T(8,128)(2,1)} fusion(bf16[256,1024]{1,0:T(8,128)(2,1)S(1)} %bitcast.36, bf16[256,256]{1,0:T(8,128)(2,1)} %reduce-scatter.7.cloned.1.call-done), kind=kOutput, calls=%fused_computation | convolution fusion | flops 134676480 | bytes 1179648 | tf_op jit(solution)/shard_map/dot_general | solution.py:54
  109.9 0.0 reduce-scatter.11.cloned.1.call-update
  109.9 0.0 reduce-scatter.9.cloned.1.call-start
  109.9 21.9 %reduce-scatter.5.cloned.1.call-done = bf16[256,256]{1,0:T(8,128)(2,1)} async-done(((bf16[1024,256]{1,0:T(8,128)(2,1)}), bf16[256,256]{1,0:T(8,128)(2,1)}) %reduce-scatter.5.cloned.1.call-update) | async-done | bytes 131088 | tf_op jit(solution)/shard_map/reduce_scatter | solution.py:45
  131.9 2.1 %convolution_convert_fusion.1 = bf16[1024,256]{1,0:T(8,128)(2,1)} fusion(bf16[256,1024]{1,0:T(8,128)(2,1)S(1)} %bitcast.35, bf16[256,256]{1,0:T(8,128)(2,1)} %reduce-scatter.5.cloned.1.call-done), kind=kOutput, calls=%fused_computation.1 | convolution fusion | flops 134676480 | bytes 1179648 | tf_op jit(solution)/shard_map/dot_general | solution.py:54
  133.9 0.9 copy-done.3
  134.8 0.9 copy-done.4
  135.7 0.7 pad_maximum_fusion.1
  136.5 19.3 %reduce-scatter.11.cloned.1.call-done = bf16[256,256]{1,0:T(8,128)(2,1)} async-done(((bf16[1024,256]{1,0:T(8,128)(2,1)}), bf16[256,256]{1,0:T(8,128)(2,1)}) %reduce-scatter.11.cloned.1.call-update) | async-done | bytes 131088 | tf_op jit(solution)/shard_map/reduce_scatter | solution.py:61
  155.7 22.8 %reduce-scatter.9.cloned.1.call-done = bf16[256,256]{1,0:T(8,128)(2,1)} async-done(((bf16[1024,256]{1,0:T(8,128)(2,1)}), bf16[256,256]{1,0:T(8,128)(2,1)}) %reduce-scatter.9.cloned.1.call-update) | async-done | bytes 131088 | tf_op jit(solution)/shard_map/reduce_scatter | solution.py:61
  178.5 1.0 fusion.1
  179.5 0.8 pad_maximum_fusion
  (15 shorter events, 0.1 us)
Async XLA Ops:
  7.2 76.4 %copy-start = (bf16[256,256]{1,0:T(8,128)(2,1)S(1)}, bf16[256,256]{1,0:T(8,128)(2,1)}, u32[]{:S(2)}) copy-start(bf16[256,256]{1,0:T(8,128)(2,1)} %param.4) | copy-start | bytes 393220
  7.2 22.0 %all-gather.2.cloned.1.call-start = ((), (), s32[]{:S(2)}) async-start(), calls=%async_computation.4 | async-start | bytes 1310720 | tf_op jit(solution)/shard_map/all_gather | solution.py:22
  7.9 75.6 %all-reduce.2.cloned.1.call-start = ((), (), s32[]{:S(2)}) async-start(), calls=%async_computation.5 | async-start | bytes 2097152 | tf_op jit(solution)/shard_map/psum | solution.py:13
  8.0 0.7 copy-start.6
  31.5 76.3 %reduce-scatter.7.cloned.1.call-start = ((), (), s32[]{:S(2)}) async-start(), calls=%async_computation.7 | async-start | bytes 655360 | tf_op jit(solution)/shard_map/reduce_scatter | solution.py:45
  83.5 2.4 %copy-start.2 = (bf16[2,256,1024]{2,1,0:T(8,128)(2,1)S(1)}, bf16[2,256,1024]{2,1,0:T(8,128)(2,1)}, u32[]{:S(2)}) copy-start(bf16[2,256,1024]{2,1,0:T(8,128)(2,1)} %all-reduce.2.cloned.1.call-done) | copy-start | bytes 3145732
  85.8 1.3 copy-start.1
  85.8 46.0 %reduce-scatter.5.cloned.1.call-start = ((), (), s32[]{:S(2)}) async-start(), calls=%async_computation.6 | async-start | bytes 655360 | tf_op jit(solution)/shard_map/reduce_scatter | solution.py:45
  87.1 68.7 %reduce-scatter.11.cloned.1.call-start = ((), (), s32[]{:S(2)}) async-start(), calls=%async_computation.9 | async-start | bytes 655360 | tf_op jit(solution)/shard_map/reduce_scatter | solution.py:61
  109.9 68.6 %reduce-scatter.9.cloned.1.call-start = ((), (), s32[]{:S(2)}) async-start(), calls=%async_computation.8 | async-start | bytes 655360 | tf_op jit(solution)/shard_map/reduce_scatter | solution.py:61
  133.9 0.9 copy-start.3
  134.8 0.9 copy-start.4
  134.8 43.7 %copy-start.5 = (f32[2,256,256]{2,1,0:T(8,128)S(1)}, f32[2,256,256]{2,1,0:T(8,128)}, u32[]{:S(2)}) copy-start(f32[2,256,256]{2,1,0:T(8,128)} %param.6) | copy-start | bytes 1572868
Sparse Core Ops, SparseCore 0:
  9.6 19.5 all-gather.1
  31.6 51.8 all-reduce.1
  86.7 21.0 reduce-scatter.6
  110.1 21.6 reduce-scatter.4
  134.1 21.6 reduce-scatter.10
  158.6 19.9 reduce-scatter.8
where the time goes:
time: 188 us; the launch traced here: 187 us
  waiting for transfers between devices  157 us (84%)
  between operations  14.2 us (8%)
  matrix products  7.57 us (4%)
  other arithmetic  5.21 us (3%)
  local copies, waits for them, and re-layouts  2.6 us (1%)
    psum x1, waiting for transfers between devices, spread(): return lax.psum(jnp.where(mine, x, jnp.zeros_like(x)), axis)  51.9 us
    reduce_scatter x2, waiting for transfers between devices, body(): lax.psum_scatter(column_term(jnp.int32(0), lax.axis_size('col') * width_p...  42.3 us
    reduce_scatter x2, waiting for transfers between devices, body(): lax.psum_scatter(diagonal_term(jnp.int32(0), lax.axis_size('row') * (full...  42 us
    all_gather x1, waiting for transfers between devices, body(): full_width = lax.all_gather(factor, 'col', axis=2, tiled=True)  20.3 us
    dot_general x2, matrix products, diagonal_term(): lax.dot_general(factor_rows, cross_block, (((0,), (1,)), ((), ())), prefe...  4.12 us
  transfers between devices with their start and end apart: 6, of which 6 were waited for; matrix products, arithmetic and copies ran while one was open for 3% of the time, Pallas kernels for 0%

commit v1 on v0

--- a/solution.py
+++ b/solution.py
@@ -10,7 +10,7 @@
 
 def spread(x, axis, root):
     mine = lax.axis_index(axis) == root
-    return lax.psum(jnp.where(mine, x, jnp.zeros_like(x)), axis)
+    return jnp.sum(lax.all_gather(jnp.where(mine, x, jnp.zeros_like(x)), axis), axis=0)
 
 
 def body(ainv_cc, factor, inv_pivot, pattern):

time: 188 us -> 217 us (1.15)
  waiting for transfers between devices: 157 us -> 185 us
  other arithmetic: 5.21 us -> 11.2 us
  local copies, waits for them, and re-layouts: 2.6 us -> 0.18 us
    all_gather x0 -> x1, waiting for transfers between devices: none -> 80.9 us  [spread(): lax.all_gather(jnp.where(mine, x, jnp.zeros_like(x)), axis)]
    psum x1 -> x0, waiting for transfers between devices: 51.9 us -> none  [spread(): return lax.psum(jnp.where(mine, x, jnp.zeros_like(x)), axis)]
    reduce_sum x0 -> x1, other arithmetic: none -> 3.43 us  [spread(): jnp.sum(lax.all_gather(jnp.where(mine, x, jnp.zeros_like(x)), axis), axis=0)]
    unnamed x16 -> x8, local copies, waits for them, and re-layouts: 2.53 us -> 0.11 us
  transfers between devices with their start and end apart: 6 -> 6, of which waited for: 6 -> 6; matrix products, arithmetic and copies ran while one was open for 3% -> 4% of each run, Pallas kernels for 0% -> 0%
where the time goes in v1:
time: 217 us
  waiting for transfers between devices  185 us (85%)
  between operations  14.2 us (7%)
  other arithmetic  11.2 us (5%)
  matrix products  6.44 us (3%)
    all_gather x1, waiting for transfers between devices, spread(): lax.all_gather(jnp.where(mine, x, jnp.zeros_like(x)), axis)  80.9 us
    reduce_scatter x2, waiting for transfers between devices, body(): lax.psum_scatter(diagonal_term(jnp.int32(0), lax.axis_size('row') * (full...  41.9 us
    reduce_scatter x2, waiting for transfers between devices, body(): lax.psum_scatter(column_term(jnp.int32(0), lax.axis_size('col') * width_p...  40.8 us
    all_gather x1, waiting for transfers between devices, body(): full_width = lax.all_gather(factor, 'col', axis=2, tiled=True)  20.3 us
    another operation x5, other arithmetic, body(): return (jnp.stack(cross_list), jnp.stack(diag_list))  4.43 us
  transfers between devices with their start and end apart: 6, of which 6 were waited for; matrix products, arithmetic and copies ran while one was open for 4% of the time, Pallas kernels for 0%

profile of v1, /device:TPU:0, one launch (start us, length us, event | category | flops | bytes accessed | tf_op | source)
XLA Modules:
  0.0 216.9 jit_solution(11503980913342985078)
XLA Ops:
  7.2 0.0 all-gather.4.cloned.1.call-start
  7.2 0.7 all-gather.4.cloned.1.call-update
  7.9 0.0 all-gather.6.cloned.1.call-start
  8.0 0.8 dynamic-slice_compare_fusion
  8.7 0.1 broadcast_bitcast_fusion
  8.8 20.3 %all-gather.4.cloned.1.call-done = bf16[2,256,1024]{2,1,0:T(8,128)(2,1)} async-done(((bf16[2,256,256]{2,1,0:T(8,128)(2,1)}), bf16[2,256,1024]{2,1,0:T(8,128)(2,1)}) %all-gather.4.cloned.1.call-update) | async-done | bytes 1048592 | tf_op jit(solution)/shard_map/all_gather | solution.py:22
  29.1 2.4 %select_select_fusion = bf16[2,256,1024]{2,1,0:T(8,128)(2,1)} fusion(bf16[2,256,1024]{2,1,0:T(8,128)(2,1)} %all-gather.4.cloned.1.call-done, pred[2,256]{1,0:T(4,128)(4,1)S(1)} %bitcast.39, pred[]{:T(512)S(6)} %eq.3), kind=kLoop, calls=%fused_computation.4 | loop fusion | flops 1048576 | bytes 2097665 | tf_op jit(solution)/shard_map/jit(_where)/select_n | solution.py:13
  31.5 0.0 all-gather.6.cloned.1.call-update
  31.6 0.0 reduce-scatter.7.cloned.1.call-start
  31.6 80.9 %all-gather.6.cloned.1.call-done = bf16[8,256,1024]{2,1,0:T(8,128)(2,1)} async-done(((bf16[2,256,1024]{2,1,0:T(8,128)(2,1)}), bf16[8,256,1024]{2,1,0:T(8,128)(2,1)}) %all-gather.6.cloned.1.call-update) | async-done | bytes 4194320 | tf_op jit(solution)/shard_map/all_gather | solution.py:13
  112.5 3.4 %reduce_sum.12 = bf16[2,256,1024]{2,1,0:T(8,128)(2,1)S(1)} reduce(bf16[4,2,256,1024]{3,2,1,0:T(8,128)(2,1)} %bitcast.36, bf16[]{:T(256)} %constant.18.clone.1), dimensions={0}, to_apply=%region_0.1 | reduce | flops 1572864 | bytes 5242882 | tf_op jit(solution)/shard_map/reduce_sum | solution.py:13
  115.9 1.1 convolution_convert_fusion.2
  117.1 0.0 reduce-scatter.7.cloned.1.call-update
  117.1 0.0 reduce-scatter.5.cloned.1.call-start
  117.2 1.2 convolution_convert_fusion.3
  118.3 0.0 reduce-scatter.5.cloned.1.call-update
  118.3 0.0 reduce-scatter.11.cloned.1.call-start
  118.4 0.1 broadcast_select_fusion
  118.6 0.1 fusion.4
  118.6 18.8 %reduce-scatter.7.cloned.1.call-done = bf16[256,256]{1,0:T(8,128)(2,1)} async-done(((bf16[1024,256]{1,0:T(8,128)(2,1)}), bf16[256,256]{1,0:T(8,128)(2,1)}) %reduce-scatter.7.cloned.1.call-update) | async-done | bytes 131088 | tf_op jit(solution)/shard_map/reduce_scatter | solution.py:45
  137.5 2.1 convolution_convert_fusion
  139.5 0.0 reduce-scatter.11.cloned.1.call-update
  139.6 0.0 reduce-scatter.9.cloned.1.call-start
  139.6 22.0 %reduce-scatter.5.cloned.1.call-done = bf16[256,256]{1,0:T(8,128)(2,1)} async-done(((bf16[1024,256]{1,0:T(8,128)(2,1)}), bf16[256,256]{1,0:T(8,128)(2,1)}) %reduce-scatter.5.cloned.1.call-update) | async-done | bytes 131088 | tf_op jit(solution)/shard_map/reduce_scatter | solution.py:45
  161.6 2.1 convolution_convert_fusion.1
  163.7 0.9 fusion.3
  164.6 0.9 fusion.2
  165.6 0.7 pad_maximum_fusion.1
  166.3 19.2 %reduce-scatter.11.cloned.1.call-done = bf16[256,256]{1,0:T(8,128)(2,1)} async-done(((bf16[1024,256]{1,0:T(8,128)(2,1)}), bf16[256,256]{1,0:T(8,128)(2,1)}) %reduce-scatter.11.cloned.1.call-update) | async-done | bytes 131088 | tf_op jit(solution)/shard_map/reduce_scatter | solution.py:61
  185.5 22.7 %reduce-scatter.9.cloned.1.call-done = bf16[256,256]{1,0:T(8,128)(2,1)} async-done(((bf16[1024,256]{1,0:T(8,128)(2,1)}), bf16[256,256]{1,0:T(8,128)(2,1)}) %reduce-scatter.9.cloned.1.call-update) | async-done | bytes 131088 | tf_op jit(solution)/shard_map/reduce_scatter | solution.py:61
  208.2 1.0 fusion.1
  209.2 0.8 pad_maximum_fusion
  (8 shorter events, 0.0 us)
Async XLA Ops:
  7.2 108.8 %copy-start = (bf16[256,256]{1,0:T(8,128)(2,1)S(1)}, bf16[256,256]{1,0:T(8,128)(2,1)}, u32[]{:S(2)}) copy-start(bf16[256,256]{1,0:T(8,128)(2,1)} %param.4) | copy-start | bytes 393220
  7.2 22.0 %all-gather.4.cloned.1.call-start = ((), (), s32[]{:S(2)}) async-start(), calls=%async_computation.4 | async-start | bytes 1310720 | tf_op jit(solution)/shard_map/all_gather | solution.py:22
  7.9 104.6 %all-gather.6.cloned.1.call-start = ((), (), s32[]{:S(2)}) async-start(), calls=%async_computation.9 | async-start | bytes 5242880 | tf_op jit(solution)/shard_map/all_gather | solution.py:13
  31.6 105.9 %reduce-scatter.7.cloned.1.call-start = ((), (), s32[]{:S(2)}) async-start(), calls=%async_computation.6 | async-start | bytes 655360 | tf_op jit(solution)/shard_map/reduce_scatter | solution.py:45
  112.5 5.9 %copy-start.1 = (bf16[2,256,1024]{2,1,0:T(8,128)(2,1)S(1)}, bf16[2,256,1024]{2,1,0:T(8,128)(2,1)}, u32[]{:S(2)}) copy-start(bf16[2,256,1024]{2,1,0:T(8,128)(2,1)} %all-gather.4.cloned.1.call-done) | copy-start | bytes 3145732
  117.1 44.5 %reduce-scatter.5.cloned.1.call-start = ((), (), s32[]{:S(2)}) async-start(), calls=%async_computation.5 | async-start | bytes 655360 | tf_op jit(solution)/shard_map/reduce_scatter | solution.py:45
  118.3 67.1 %reduce-scatter.11.cloned.1.call-start = ((), (), s32[]{:S(2)}) async-start(), calls=%async_computation.8 | async-start | bytes 655360 | tf_op jit(solution)/shard_map/reduce_scatter | solution.py:61
  118.4 89.8 %copy-start.2 = (f32[2,256,256]{2,1,0:T(8,128)S(1)}, f32[2,256,256]{2,1,0:T(8,128)}, u32[]{:S(2)}) copy-start(f32[2,256,256]{2,1,0:T(8,128)} %param.6) | copy-start | bytes 1572868
  139.6 68.6 %reduce-scatter.9.cloned.1.call-start = ((), (), s32[]{:S(2)}) async-start(), calls=%async_computation.7 | async-start | bytes 655360 | tf_op jit(solution)/shard_map/reduce_scatter | solution.py:61
Sparse Core Ops, SparseCore 0:
  9.6 19.5 all-gather.3
  31.7 80.7 all-gather.5
  117.2 20.1 reduce-scatter.6
  140.0 21.6 reduce-scatter.4
  163.8 21.6 reduce-scatter.10
  188.2 19.9 reduce-scatter.8
